TPU v7x, 32 devices: a whole 2x2x4 slice. The times are simulated.
32 devices in a mesh: fsdp: 4 (over y, x), ctx: 4 (over z), tp: 2 (over core).
Axes of the slice: x: 2, y: 2, z: 4, core: 2. Of those that a mesh axis runs over, the one named last changes fastest.
Arguments:
- tokens: bfloat16 [8, 2048, 768], P('fsdp', 'ctx'), may hold values from -6 to 6
- doc_lengths: int32 [8, 8], P('fsdp'), may hold values from 1 to 1536, 2048 in all within a row
- keep: int32 [8, 2048], P('fsdp', 'ctx'), may hold values 0 or 1
- w_query: bfloat16 [768, 768], P('fsdp', 'tp'), may hold values from -0.21875 to 0.21875
- b_query: float32 [768], P('tp'), may hold values from -3 to 3
- w_key: bfloat16 [768, 768], P('fsdp', 'tp'), may hold values from -0.21875 to 0.21875
- w_value: bfloat16 [768, 768], P('fsdp', 'tp'), may hold values from -0.21875 to 0.21875
- b_value: float32 [768], P('tp'), may hold values from -3 to 3
- w_out: bfloat16 [768, 768], P('fsdp', 'tp'), may hold values from -0.4375 to 0.4375
- b_out: float32 [768], replicated, may hold values from -3 to 3
- gain_one: float32 [768], replicated, may hold values from 0.5 to 1.5
- shift_one: float32 [768], replicated, may hold values from -2 to 2
- w_up: bfloat16 [768, 2, 3072], P('fsdp', None, 'tp'), may hold values from -0.21875 to 0.21875
- w_down: bfloat16 [768, 3072], P('fsdp', 'tp'), may hold values from -0.15625 to 0.15625
- b_down: float32 [768], replicated, may hold values from -3 to 3
- gain_two: float32 [768], replicated, may hold values from 0.5 to 1.5
- shift_two: float32 [768], replicated, may hold values from -2 to 2
- cotangent: bfloat16 [8, 2048, 768], P('fsdp', 'ctx'), may hold values from -6 to 6
Outputs:
- out: bfloat16 [8, 2048, 768], P('fsdp', 'ctx')
- d_tokens: float32 [8, 2048, 768], P('fsdp', 'ctx')
- d_w_query: float32 [768, 768], P('fsdp', 'tp')
- d_b_query: float32 [768], P('tp')
- d_w_key: float32 [768, 768], P('fsdp', 'tp')
- d_w_value: float32 [768, 768], P('fsdp', 'tp')
- d_b_value: float32 [768], P('tp')
- d_w_out: float32 [768, 768], P('fsdp', 'tp')
- d_b_out: float32 [768], replicated
- d_gain_one: float32 [768], replicated
- d_shift_one: float32 [768], replicated
- d_w_up: float32 [768, 2, 3072], P('fsdp', None, 'tp')
- d_w_down: float32 [768, 3072], P('fsdp', 'tp')
- d_b_down: float32 [768], replicated
- d_gain_two: float32 [768], replicated
- d_shift_two: float32 [768], replicated
Inputs may be any that keep to these rules, and one draw needn't show every extreme that they name: `doc_lengths`: row b lists the lengths of the 8 documents of sequence b in order; they sum to 2048. `keep`: 0 marks a padding token, which only itself attends to.
All inputs are finite; a program needn't handle non-finite values. No bound on the sum of `keep` on one device may be relied on, other than what follows from the above.
Results may differ from a plain program's by a relative error of at most 0.029.
Values may be sent and summed in bfloat16 or wider, within the bound.
A program may use at most 256 MiB of HBM per device.

v0:
```python
import jax
import jax.numpy as jnp
from jax import lax
from jax.sharding import PartitionSpec as P

HEAD = 64
NORM_EPS = 1e-12
MASKED = -1e30


def layer_norm(residual, norm_gain, norm_shift):
    centered = residual - jnp.mean(residual, -1, keepdims=True)
    inv_scale = lax.rsqrt(jnp.mean(centered * centered, -1, keepdims=True) + NORM_EPS)
    normed = centered * inv_scale
    return (normed * norm_gain + norm_shift, normed, inv_scale)


def norm_back(grad_out, normed, inv_scale, norm_gain):
    grad_norm = grad_out * norm_gain
    mean_grad = jnp.mean(grad_norm, -1, keepdims=True)
    mean_cross = jnp.mean(grad_norm * normed, -1, keepdims=True)
    grad_in = (grad_norm - mean_grad - normed * mean_cross) * inv_scale
    return (grad_in, jnp.sum(grad_out * normed, 0), jnp.sum(grad_out, 0))


def head_slopes(first_head, head_count):
    head_index = first_head + jnp.arange(head_count, dtype=jnp.int32)
    head_float = head_index.astype(jnp.float32)
    return jnp.where(head_index < 8, jnp.exp2(-(head_float + 1.0)), jnp.exp2(-(head_float - 7.5)))


def segment_ids(lengths, positions):
    bounds = jnp.cumsum(lengths, -1)
    return jnp.sum((bounds[:, None, :] <= positions[None, :, None]).astype(jnp.int32), -1)


def score_block(query_heads, query_pos, query_seg, key_heads, key_pos, key_seg, key_keep, slopes):
    scores = (
        jnp.einsum("sqhd,skhd->shqk", query_heads, key_heads, preferred_element_type=jnp.float32)
        * 0.125
    )
    distance = jnp.abs(query_pos[:, None] - key_pos[None, :]).astype(jnp.float32)
    scores = scores - slopes[None, :, None, None] * distance[None, None]
    same_doc = query_seg[:, None, :, None] == key_seg[:, None, None, :]
    visible = (key_keep[:, None, None, :] == 1) | (query_pos[:, None] == key_pos[None, :])[
        None, None
    ]
    return (scores, same_doc & visible)


def grad_block(
    query_heads,
    query_pos,
    query_seg,
    grad_heads,
    log_total,
    delta,
    key_heads,
    value_heads,
    key_pos,
    key_seg,
    key_keep,
    slopes,
):
    scores, allowed = score_block(
        query_heads, query_pos, query_seg, key_heads, key_pos, key_seg, key_keep, slopes
    )
    probs = jnp.where(allowed, jnp.exp(scores - log_total[..., None]), 0.0)
    grad_probs = jnp.einsum(
        "sqhd,skhd->shqk", grad_heads, value_heads, preferred_element_type=jnp.float32
    )
    grad_scores = (probs * (grad_probs - delta[..., None])).astype(jnp.bfloat16)
    grad_query = (
        jnp.einsum("shqk,skhd->sqhd", grad_scores, key_heads, preferred_element_type=jnp.float32)
        * 0.125
    )
    grad_key = (
        jnp.einsum("shqk,sqhd->skhd", grad_scores, query_heads, preferred_element_type=jnp.float32)
        * 0.125
    )
    grad_value = jnp.einsum(
        "shqk,sqhd->skhd",
        probs.astype(jnp.bfloat16),
        grad_heads,
        preferred_element_type=jnp.float32,
    )
    return (grad_query, grad_key, grad_value)


def intersections(query_seg, key_seg):
    return jnp.any((key_seg[:, 0] <= query_seg[:, -1]) & (key_seg[:, -1] >= query_seg[:, 0]))


def guarded(active, update, current):
    return lax.cond(active, update, lambda untouched: untouched, current)


def over_blocks(length, advance, current):
    block_len = 512
    block_count = length // block_len
    return lax.fori_loop(
        0,
        block_count,
        lambda block_index, running: advance(running, block_index * block_len, block_len),
        current,
    )


def per_device(
    tokens,
    doc_lengths,
    keep,
    w_query,
    b_query,
    w_key,
    w_value,
    b_value,
    w_out,
    b_out,
    gain_one,
    shift_one,
    w_up,
    w_down,
    b_down,
    gain_two,
    shift_two,
    cotangent,
):
    seq_count, block_rows, model_width = tokens.shape
    local_heads = b_query.shape[0] // HEAD
    head_width = local_heads * HEAD
    row_count = seq_count * block_rows
    slopes = head_slopes(lax.axis_index("tp") * local_heads, local_heads)
    own_pos = lax.axis_index("ctx") * block_rows + jnp.arange(block_rows, dtype=jnp.int32)
    own_seg = segment_ids(doc_lengths, own_pos)
    token_rows = tokens.reshape(row_count, model_width)
    full_query, full_key, full_value, full_out = (
        lax.all_gather(w_query, "fsdp", axis=0, tiled=True),
        lax.all_gather(w_key, "fsdp", axis=0, tiled=True),
        lax.all_gather(w_value, "fsdp", axis=0, tiled=True),
        lax.all_gather(w_out, "fsdp", axis=0, tiled=True),
    )
    queries = (
        jnp.dot(token_rows, full_query, preferred_element_type=jnp.float32) + b_query
    ).astype(jnp.bfloat16)
    key_rows = jnp.dot(token_rows, full_key, preferred_element_type=jnp.float32).astype(
        jnp.bfloat16
    )
    values = (jnp.dot(token_rows, full_value, preferred_element_type=jnp.float32) + b_value).astype(
        jnp.bfloat16
    )
    query_heads = queries.reshape(seq_count, block_rows, local_heads, HEAD)
    key_value = jnp.concatenate([key_rows, values], -1).reshape(
        seq_count, block_rows, 2 * head_width
    )

    def split_pairs(slab_pairs, block_len):
        return (
            slab_pairs[..., :head_width].reshape(seq_count, block_len, local_heads, HEAD),
            slab_pairs[..., head_width:].reshape(seq_count, block_len, local_heads, HEAD),
        )

    def key_slab(pairs, piece_keep, offset, block_len):
        slab_pairs = lax.dynamic_slice_in_dim(pairs, offset, block_len, 1)
        slab_keep = lax.dynamic_slice_in_dim(piece_keep, offset, block_len, 1)
        key_pos = offset + jnp.arange(block_len, dtype=jnp.int32)
        key_seg = segment_ids(doc_lengths, key_pos)
        slab_keys, slab_values = split_pairs(slab_pairs, block_len)
        return (slab_keys, slab_values, slab_keep, key_pos, key_seg)

    start_state = (
        jnp.full((seq_count, local_heads, block_rows), MASKED, jnp.float32),
        jnp.zeros((seq_count, local_heads, block_rows), jnp.float32),
        jnp.zeros((seq_count, local_heads, block_rows, HEAD), jnp.float32),
    )
    pairs = lax.all_gather(key_value, "ctx", axis=1, tiled=True)
    piece_keep = lax.all_gather(keep, "ctx", axis=1, tiled=True)

    def advance(partial_value, offset, block_len):
        slab_keys, slab_values, slab_keep, key_pos, key_seg = key_slab(
            pairs, piece_keep, offset, block_len
        )

        def update(current):
            row_max, row_sum, weighted = current
            scores, allowed = score_block(
                query_heads, own_pos, own_seg, slab_keys, key_pos, key_seg, slab_keep, slopes
            )
            scores = jnp.where(allowed, scores, MASKED)
            new_max = jnp.maximum(row_max, jnp.max(scores, -1))
            factor = jnp.exp(row_max - new_max)
            weights = jnp.where(allowed, jnp.exp(scores - new_max[..., None]), 0.0)
            row_sum = row_sum * factor + jnp.sum(weights, -1)
            weighted = weighted * factor[..., None] + jnp.einsum(
                "shqk,skhd->shqd",
                weights.astype(jnp.bfloat16),
                slab_values,
                preferred_element_type=jnp.float32,
            )
            return (new_max, row_sum, weighted)

        return guarded(intersections(own_seg, key_seg), update, partial_value)

    row_max, row_sum, weighted = over_blocks(pairs.shape[1], advance, start_state)
    attended = (
        (weighted / row_sum[..., None])
        .transpose(0, 2, 1, 3)
        .reshape(row_count, head_width)
        .astype(jnp.bfloat16)
    )
    log_total = row_max + jnp.log(row_sum)
    att_part = jnp.einsum("rh,dh->rd", attended, full_out, preferred_element_type=jnp.float32)
    branch_att = lax.psum(att_part.astype(jnp.bfloat16), "tp").astype(jnp.float32) + b_out
    first_out, normed_one, inv_one = layer_norm(
        token_rows.astype(jnp.float32) + branch_att, gain_one, shift_one
    )
    first_low = first_out.astype(jnp.bfloat16)
    full_up, full_down = (
        lax.all_gather(w_up, "fsdp", axis=0, tiled=True),
        lax.all_gather(w_down, "fsdp", axis=0, tiled=True),
    )
    gate_up = jnp.einsum("rd,dcf->rcf", first_low, full_up, preferred_element_type=jnp.float32)
    product, gelu_back = jax.vjp(
        lambda gate_part, up_part: jax.nn.gelu(gate_part, approximate=False) * up_part,
        gate_up[:, 0],
        gate_up[:, 1],
    )
    hidden = product.astype(jnp.bfloat16)
    ffn_part = jnp.einsum("rf,df->rd", hidden, full_down, preferred_element_type=jnp.float32)
    branch_ffn = lax.psum(ffn_part.astype(jnp.bfloat16), "tp").astype(jnp.float32) + b_down
    result, normed_two, inv_two = layer_norm(first_out + branch_ffn, gain_two, shift_two)
    grad_in = cotangent.reshape(row_count, model_width).astype(jnp.float32)
    grad_two, d_gain_two, d_shift_two = norm_back(grad_in, normed_two, inv_two, gain_two)
    grad_ffn = grad_two.astype(jnp.bfloat16)
    d_b_down = jnp.sum(grad_ffn.astype(jnp.float32), 0)
    d_w_down = jnp.einsum("rd,rf->df", grad_ffn, hidden, preferred_element_type=jnp.float32)
    grad_hidden = jnp.einsum("rd,df->rf", grad_ffn, full_down, preferred_element_type=jnp.float32)
    grad_gate, grad_up = gelu_back(grad_hidden)
    grad_gate_up = jnp.stack([grad_gate, grad_up], 1).astype(jnp.bfloat16)
    d_w_up = jnp.einsum("rd,rcf->dcf", first_low, grad_gate_up, preferred_element_type=jnp.float32)
    first_part = jnp.einsum(
        "rcf,dcf->rd", grad_gate_up, full_up, preferred_element_type=jnp.float32
    )
    grad_first = grad_two + lax.psum(first_part.astype(jnp.bfloat16), "tp").astype(jnp.float32)
    grad_one, d_gain_one, d_shift_one = norm_back(grad_first, normed_one, inv_one, gain_one)
    grad_att = grad_one.astype(jnp.bfloat16)
    d_b_out = jnp.sum(grad_att.astype(jnp.float32), 0)
    d_w_out = jnp.einsum("rd,rh->dh", grad_att, attended, preferred_element_type=jnp.float32)
    grad_attended = jnp.einsum(
        "rd,dh->rh", grad_att, full_out, preferred_element_type=jnp.float32
    ).astype(jnp.bfloat16)
    grad_heads = grad_attended.reshape(seq_count, block_rows, local_heads, HEAD)
    delta = jnp.einsum(
        "sqhd,sqhd->shq",
        grad_heads,
        attended.reshape(seq_count, block_rows, local_heads, HEAD),
        preferred_element_type=jnp.float32,
    )
    query_zero = jnp.zeros((seq_count, block_rows, local_heads, HEAD), jnp.float32)
    full_len = block_rows * lax.axis_size("ctx")
    term_zero = jnp.zeros((seq_count, full_len, 2 * head_width), jnp.float32)
    return_pairs = lax.all_gather(key_value, "ctx", axis=1, tiled=True)
    return_piece_keep = lax.all_gather(keep, "ctx", axis=1, tiled=True)

    def advance(partial_value, offset, block_len):
        slab_keys, slab_values, slab_keep, key_pos, key_seg = key_slab(
            return_pairs, return_piece_keep, offset, block_len
        )

        def update(current):
            query_grad, key_terms = current
            part_query, part_key, part_value = grad_block(
                query_heads,
                own_pos,
                own_seg,
                grad_heads,
                log_total,
                delta,
                slab_keys,
                slab_values,
                key_pos,
                key_seg,
                slab_keep,
                slopes,
            )
            slab_grads = jnp.concatenate(
                [
                    part_key.reshape(seq_count, block_len, head_width),
                    part_value.reshape(seq_count, block_len, head_width),
                ],
                -1,
            )
            return (
                query_grad + part_query,
                lax.dynamic_update_slice_in_dim(key_terms, slab_grads, offset, 1),
            )

        return guarded(intersections(own_seg, key_seg), update, partial_value)

    query_grad, key_terms = over_blocks(return_pairs.shape[1], advance, (query_zero, term_zero))
    pair_grads = lax.psum_scatter(
        key_terms.astype(jnp.bfloat16), "ctx", scatter_dimension=1, tiled=True
    ).astype(jnp.float32)
    query_low = query_grad.reshape(row_count, head_width).astype(jnp.bfloat16)
    pair_low = pair_grads.reshape(row_count, 2 * head_width).astype(jnp.bfloat16)
    grad_project = jnp.concatenate([query_low, pair_low], -1)
    joined_weights = jnp.concatenate([full_query, full_key, full_value], -1)
    joined_grads = jnp.einsum(
        "rd,rh->dh", token_rows, grad_project, preferred_element_type=jnp.float32
    )
    input_part = jnp.einsum(
        "rh,dh->rd", grad_project, joined_weights, preferred_element_type=jnp.float32
    )
    d_tokens = grad_one + lax.psum(input_part.astype(jnp.bfloat16), "tp").astype(jnp.float32)
    d_b_query = jnp.sum(query_low.astype(jnp.float32), 0)
    d_b_value = jnp.sum(pair_low[:, head_width:].astype(jnp.float32), 0)
    d_w_query = joined_grads[:, :head_width]
    d_w_key = joined_grads[:, head_width : 2 * head_width]
    d_w_value = joined_grads[:, 2 * head_width :]
    shard_grads = (
        lax.psum_scatter(
            d_w_query.astype(jnp.bfloat16), "fsdp", scatter_dimension=0, tiled=True
        ).astype(jnp.float32),
        lax.psum_scatter(
            d_w_key.astype(jnp.bfloat16), "fsdp", scatter_dimension=0, tiled=True
        ).astype(jnp.float32),
        lax.psum_scatter(
            d_w_value.astype(jnp.bfloat16), "fsdp", scatter_dimension=0, tiled=True
        ).astype(jnp.float32),
        lax.psum_scatter(
            d_w_out.astype(jnp.bfloat16), "fsdp", scatter_dimension=0, tiled=True
        ).astype(jnp.float32),
        lax.psum_scatter(
            d_w_up.astype(jnp.bfloat16), "fsdp", scatter_dimension=0, tiled=True
        ).astype(jnp.float32),
        lax.psum_scatter(
            d_w_down.astype(jnp.bfloat16), "fsdp", scatter_dimension=0, tiled=True
        ).astype(jnp.float32),
    )
    sum_query, sum_key, sum_value, sum_out, sum_up, sum_down = (
        lax.psum(shard_grads[0].astype(jnp.bfloat16), "ctx").astype(jnp.float32),
        lax.psum(shard_grads[1].astype(jnp.bfloat16), "ctx").astype(jnp.float32),
        lax.psum(shard_grads[2].astype(jnp.bfloat16), "ctx").astype(jnp.float32),
        lax.psum(shard_grads[3].astype(jnp.bfloat16), "ctx").astype(jnp.float32),
        lax.psum(shard_grads[4].astype(jnp.bfloat16), "ctx").astype(jnp.float32),
        lax.psum(shard_grads[5].astype(jnp.bfloat16), "ctx").astype(jnp.float32),
    )
    (
        total_b_query,
        total_b_value,
        total_b_out,
        total_b_down,
        total_gain_one,
        total_shift_one,
        total_gain_two,
        total_shift_two,
    ) = lax.psum(
        (d_b_query, d_b_value, d_b_out, d_b_down, d_gain_one, d_shift_one, d_gain_two, d_shift_two),
        ("fsdp", "ctx"),
    )
    return (
        result.reshape(seq_count, block_rows, model_width).astype(jnp.bfloat16),
        d_tokens.reshape(seq_count, block_rows, model_width),
        sum_query,
        total_b_query,
        sum_key,
        sum_value,
        total_b_value,
        sum_out,
        total_b_out,
        total_gain_one,
        total_shift_one,
        sum_up,
        sum_down,
        total_b_down,
        total_gain_two,
        total_shift_two,
    )


def solution(mesh):
    in_specs = (
        P("fsdp", "ctx", None),
        P("fsdp", None),
        P("fsdp", "ctx"),
        P("fsdp", "tp"),
        P("tp"),
        P("fsdp", "tp"),
        P("fsdp", "tp"),
        P("tp"),
        P("fsdp", "tp"),
        P(),
        P(),
        P(),
        P("fsdp", None, "tp"),
        P("fsdp", "tp"),
        P(),
        P(),
        P(),
        P("fsdp", "ctx", None),
    )
    out_specs = (
        P("fsdp", "ctx", None),
        P("fsdp", "ctx", None),
        P("fsdp", "tp"),
        P("tp"),
        P("fsdp", "tp"),
        P("fsdp", "tp"),
        P("tp"),
        P("fsdp", "tp"),
        P(),
        P(),
        P(),
        P("fsdp", None, "tp"),
        P("fsdp", "tp"),
        P(),
        P(),
        P(),
    )
    return jax.shard_map(
        per_device, mesh=mesh, in_specs=in_specs, out_specs=out_specs, check_vma=False
    )
```

profile of v0, /device:TPU:0, one launch (start us, length us, event | category | flops | bytes accessed | tf_op | source)
XLA Modules:
  0.0 1039.2 jit_solution(15343525228402633456)
XLA Ops:
  8.1 12.4 %all_gather.28 = bf16[768,384]{1,0:T(8,128)(2,1)S(1)} all-gather(bf16[192,384]{1,0:T(8,128)(2,1)} %param.32), channel_id=1, replica_groups=mesh['fsdp'=4,'ctx'=4,'tp'=2] {'fsdp'}, dimensions={0}, use_global_device_ids=true | all-gather | bytes 737280 | tf_op jit(solution)/shard_map/all_gather | solution.py:140
  20.5 10.4 %all_gather.27 = bf16[768,384]{1,0:T(8,128)(2,1)S(1)} all-gather(bf16[192,384]{1,0:T(8,128)(2,1)} %param.31), channel_id=1, replica_groups=mesh['fsdp'=4,'ctx'=4,'tp'=2] {'fsdp'}, dimensions={0}, use_global_device_ids=true | all-gather | bytes 737280 | tf_op jit(solution)/shard_map/all_gather | solution.py:139
  36.0 9.7 all_gather.30
  48.5 13.5 %all_gather.26 = s32[2,2048]{1,0:T(2,128)S(1)} all-gather(s32[2,512]{1,0:T(2,128)S(1)} %copy-done.41), channel_id=1, replica_groups=mesh['fsdp'=4,'ctx'=4,'tp'=2] {'ctx'}, dimensions={1}, use_global_device_ids=true | all-gather | bytes 20480 | tf_op jit(solution)/shard_map/all_gather | solution.py:177
  62.0 10.8 %all_gather.31 = bf16[768,384]{1,0:T(8,128)(2,1)} all-gather(bf16[192,384]{1,0:T(8,128)(2,1)S(1)} %copy-done.26), channel_id=1, replica_groups=mesh['fsdp'=4,'ctx'=4,'tp'=2] {'fsdp'}, dimensions={0}, use_global_device_ids=true | all-gather | bytes 737280 | tf_op jit(solution)/shard_map/all_gather | solution.py:141
  72.9 78.7 %all-gather.4.cloned.1.call-done = bf16[2,2048,768]{1,2,0:T(8,128)(2,1)} async-done(((bf16[2,512,768]{1,2,0:T(8,128)(2,1)}), bf16[2,2048,768]{1,2,0:T(8,128)(2,1)}) %all-gather.4.cloned.1.call-update) | async-done | bytes 6291472 | tf_op jit(solution)/shard_map/all_gather | solution.py:176
  151.8 86.0 %while.38 = (s32[]{:T(128)}, f32[2,6,512]{2,1,0:T(8,128)S(1)}, f32[2,6,512]{2,1,0:T(8,128)S(1)}, f32[2,6,512,64]{2,3,1,0:T(8,128)S(1)}, s32[2,1,8]{2,0,1:T(2,128...) while((s32[]{:T(128)}, f32[2,6,512]{2,1,0:T(8,128)S(1)}, ...), condition=%wide.region_9.10_spmd.clone, body=%wide.region_2.9_spmd.clone.sunk | while | flops 860657216 | bytes 95593216 | solution.py:101
  153.4 20.0 %conditional.6 = ((f32[2,6,512]{2,1,0:T(8,128)S(1)}, f32[2,6,512]{2,1,0:T(8,128)S(1)}, f32[2,6,512,64]{2,3,1,0:T(8,128)S(1)})) conditional(s32[]{:T(128)} %convert_element_type.410, (f32[2,6,512]{2,1,0:T(8,128)S(1)}, f32[2,6,512]{2,1,0:T(8,128)S(1)}, f32[2,6,512,64]{2,3,1,0:T(8,128)S(1)}) %tuple.180, (s32[2,512]{1,0:T(2,128)S(1)}, ...), branch_computations={%region_5.5_spmd, %region_6.8_spmd.clone} | conditional | flops 860633152 | bytes 95582496 | solution.py:95
  159.6 5.7 fusion.11
  165.4 3.8 fusion.10
  169.2 4.1 multiply_add_fusion
  174.9 20.0 %conditional.6 = ((f32[2,6,512]{2,1,0:T(8,128)S(1)}, f32[2,6,512]{2,1,0:T(8,128)S(1)}, f32[2,6,512,64]{2,3,1,0:T(8,128)S(1)})) conditional(s32[]{:T(128)} %convert_element_type.410, (f32[2,6,512]{2,1,0:T(8,128)S(1)}, f32[2,6,512]{2,1,0:T(8,128)S(1)}, f32[2,6,512,64]{2,3,1,0:T(8,128)S(1)}) %tuple.180, (s32[2,512]{1,0:T(2,128)S(1)}, ...), branch_computations={%region_5.5_spmd, %region_6.8_spmd.clone} | conditional | flops 860633152 | bytes 95582496 | solution.py:95
  181.1 5.7 fusion.11
  186.9 3.8 fusion.10
  190.7 4.1 multiply_add_fusion
  196.4 20.0 %conditional.6 = ((f32[2,6,512]{2,1,0:T(8,128)S(1)}, f32[2,6,512]{2,1,0:T(8,128)S(1)}, f32[2,6,512,64]{2,3,1,0:T(8,128)S(1)})) conditional(s32[]{:T(128)} %convert_element_type.410, (f32[2,6,512]{2,1,0:T(8,128)S(1)}, f32[2,6,512]{2,1,0:T(8,128)S(1)}, f32[2,6,512,64]{2,3,1,0:T(8,128)S(1)}) %tuple.180, (s32[2,512]{1,0:T(2,128)S(1)}, ...), branch_computations={%region_5.5_spmd, %region_6.8_spmd.clone} | conditional | flops 860633152 | bytes 95582496 | solution.py:95
  202.6 5.7 fusion.11
  208.4 3.8 fusion.10
  212.2 4.1 multiply_add_fusion
  217.9 20.0 %conditional.6 = ((f32[2,6,512]{2,1,0:T(8,128)S(1)}, f32[2,6,512]{2,1,0:T(8,128)S(1)}, f32[2,6,512,64]{2,3,1,0:T(8,128)S(1)})) conditional(s32[]{:T(128)} %convert_element_type.410, (f32[2,6,512]{2,1,0:T(8,128)S(1)}, f32[2,6,512]{2,1,0:T(8,128)S(1)}, f32[2,6,512,64]{2,3,1,0:T(8,128)S(1)}) %tuple.180, (s32[2,512]{1,0:T(2,128)S(1)}, ...), branch_computations={%region_5.5_spmd, %region_6.8_spmd.clone} | conditional | flops 860633152 | bytes 95582496 | solution.py:95
  224.1 5.7 fusion.11
  233.7 4.1 multiply_add_fusion
  245.5 15.5 %all-reduce.8.cloned.1.call-done = bf16[1024,768]{1,0:T(8,128)(2,1)} async-done(((bf16[1024,768]{1,0:T(8,128)(2,1)}), bf16[1024,768]{1,0:T(8,128)(2,1)}) %all-reduce.8.cloned.1.call-update) | async-done | bytes 1572880 | tf_op jit(solution)/shard_map/psum | solution.py:213
  267.1 33.3 %all-gather.6.cloned.1.call-done = bf16[768,2,1536]{2,0,1:T(8,128)(2,1)} async-done(((bf16[192,2,1536]{2,0,1:T(8,128)(2,1)}), bf16[768,2,1536]{2,0,1:T(8,128)(2,1)}) %all-gather.6.cloned.1.call-update) | async-done | bytes 4718608 | tf_op jit(solution)/shard_map/all_gather | solution.py:219
  300.4 7.8 fusion.80
  308.2 4.7 copy-done.11
  312.9 14.7 %multiply_convert_fusion.1 = (bf16[1024,1536]{1,0:T(8,128)(2,1)}, f32[1024,1536]{1,0:T(8,128)}) fusion(f32[1024,2,1536]{2,0,1:T(8,128)S(1)} %fusion.80), kind=kLoop, calls=%fused_computation.88 | loop fusion | flops 103809024 | bytes 22020096 | tf_op jit(solution)/shard_map/convert_element_type | solution.py:228
  327.6 11.9 %all-gather.8.cloned.1.call-done = bf16[768,1536]{1,0:T(8,128)(2,1)} async-done(((bf16[192,1536]{1,0:T(8,128)(2,1)}), bf16[768,1536]{1,0:T(8,128)(2,1)}) %all-gather.8.cloned.1.call-update) | async-done | bytes 2359312 | tf_op jit(solution)/shard_map/all_gather | solution.py:220
  339.6 6.4 convolution_convert_fusion.4
  349.1 17.5 %all-reduce.10.cloned.1.call-done = bf16[1024,768]{1,0:T(8,128)(2,1)} async-done(((bf16[1024,768]{1,0:T(8,128)(2,1)}), bf16[1024,768]{1,0:T(8,128)(2,1)}) %all-reduce.10.cloned.1.call-update) | async-done | bytes 1572880 | tf_op jit(solution)/shard_map/psum | solution.py:230
  375.6 10.2 fusion.65
  385.7 9.5 bitcast_convert_fusion
  395.8 21.2 %all-reduce.12.cloned.1.call-done = bf16[1024,768]{1,0:T(8,128)(2,1)} async-done(((bf16[1024,768]{1,0:T(8,128)(2,1)}), bf16[1024,768]{1,0:T(8,128)(2,1)}) %all-reduce.12.cloned.1.call-update) | async-done | bytes 1572880 | tf_op jit(solution)/shard_map/psum | solution.py:244
  417.0 6.1 multiply_reduce_fusion
  443.3 136.7 %while.39 = (s32[]{:T(128)}, f32[2,512,6,64]{1,3,2,0:T(8,128)}, bf16[2,2048,768]{1,2,0:T(8,128)(2,1)}, s32[2,1,8]{2,0,1:T(2,128)S(1)}, s32[2,512]{1,0:T(2,128)S(...) while((s32[]{:T(128)}, f32[2,512,6,64]{1,3,2,0:T(8,128)}, ...), condition=%wide.region_26.27_spmd.clone, body=%wide.region_21.0_spmd.clone.sunk | while | flops 2059953664 | bytes 96322272 | solution.py:101
  444.9 32.6 %conditional.7 = ((f32[2,512,6,64]{1,3,2,0:T(8,128)}, bf16[2,2048,768]{1,2,0:T(8,128)(2,1)})) conditional(s32[]{:T(128)} %convert_element_type.412, (f32[2,512,6,64]{1,3,2,0:T(8,128)}, bf16[2,2048,768]{1,2,0:T(8,128)(2,1)}) %tuple.184, (s32[2,512]{1,0:T(2,128)S(1)}, s32[2,512]{1,0:T(2,128)S(1)}, s32[]{:T(128)}, s32[2,2048]{1,0:T(2,128)S(1)}, ...), branch_computations={%region_24.24_spmd, %region_25.25_spmd.clone} | conditional | flops 2059929600 | bytes 96311528 | solution.py:95
  448.3 6.4 fusion.98
  455.9 8.2 fusion.23
  466.1 6.5 fusion.28
  479.0 32.7 %conditional.7 = ((f32[2,512,6,64]{1,3,2,0:T(8,128)}, bf16[2,2048,768]{1,2,0:T(8,128)(2,1)})) conditional(s32[]{:T(128)} %convert_element_type.412, (f32[2,512,6,64]{1,3,2,0:T(8,128)}, bf16[2,2048,768]{1,2,0:T(8,128)(2,1)}) %tuple.184, (s32[2,512]{1,0:T(2,128)S(1)}, s32[2,512]{1,0:T(2,128)S(1)}, s32[]{:T(128)}, s32[2,2048]{1,0:T(2,128)S(1)}, ...), branch_computations={%region_24.24_spmd, %region_25.25_spmd.clone} | conditional | flops 2059929600 | bytes 96311528 | solution.py:95
  482.4 6.4 fusion.98
  489.9 8.2 fusion.23
  500.2 6.5 fusion.28
  513.2 32.6 %conditional.7 = ((f32[2,512,6,64]{1,3,2,0:T(8,128)}, bf16[2,2048,768]{1,2,0:T(8,128)(2,1)})) conditional(s32[]{:T(128)} %convert_element_type.412, (f32[2,512,6,64]{1,3,2,0:T(8,128)}, bf16[2,2048,768]{1,2,0:T(8,128)(2,1)}) %tuple.184, (s32[2,512]{1,0:T(2,128)S(1)}, s32[2,512]{1,0:T(2,128)S(1)}, s32[]{:T(128)}, s32[2,2048]{1,0:T(2,128)S(1)}, ...), branch_computations={%region_24.24_spmd, %region_25.25_spmd.clone} | conditional | flops 2059929600 | bytes 96311528 | solution.py:95
  516.5 6.4 fusion.98
  524.1 8.2 fusion.23
  534.3 6.5 fusion.28
  547.3 32.7 %conditional.7 = ((f32[2,512,6,64]{1,3,2,0:T(8,128)}, bf16[2,2048,768]{1,2,0:T(8,128)(2,1)})) conditional(s32[]{:T(128)} %convert_element_type.412, (f32[2,512,6,64]{1,3,2,0:T(8,128)}, bf16[2,2048,768]{1,2,0:T(8,128)(2,1)}) %tuple.184, (s32[2,512]{1,0:T(2,128)S(1)}, s32[2,512]{1,0:T(2,128)S(1)}, s32[]{:T(128)}, s32[2,2048]{1,0:T(2,128)S(1)}, ...), branch_computations={%region_24.24_spmd, %region_25.25_spmd.clone} | conditional | flops 2059929600 | bytes 96311528 | solution.py:95
  550.6 6.4 fusion.98
  558.2 8.2 fusion.23
  568.4 6.5 fusion.28
  579.9 8.7 copy.101
  591.9 108.8 %reduce-scatter.14.cloned.1.call-done = bf16[2,512,768]{2,1,0:T(8,128)(2,1)} async-done(((bf16[2,2048,768]{2,1,0:T(8,128)(2,1)}), bf16[2,512,768]{2,1,0:T(8,128)(2,1)}) %reduce-scatter.14.cloned.1.call-update) | async-done | bytes 1572880 | tf_op jit(solution)/shard_map/reduce_scatter | solution.py:301
  715.3 6.9 convolution_convert_fusion.1
  722.3 9.8 convolution_convert_fusion
  732.1 5.6 fusion.75
  739.8 22.1 %reduce-scatter.24.cloned.1.call-done = bf16[192,384]{1,0:T(8,128)(2,1)} async-done(((bf16[768,384]{1,0:T(8,128)(2,1)}), bf16[192,384]{1,0:T(8,128)(2,1)}) %reduce-scatter.24.cloned.1.call-update) | async-done | bytes 147472
  763.6 26.4 %reduce-scatter.26.cloned.1.call-done = bf16[192,384]{1,0:T(8,128)(2,1)} async-done(((bf16[768,384]{1,0:T(8,128)(2,1)}), bf16[192,384]{1,0:T(8,128)(2,1)}) %reduce-scatter.26.cloned.1.call-update) | async-done | bytes 147472
  791.7 26.6 %reduce-scatter.16.cloned.1.call-done = bf16[192,384]{1,0:T(8,128)(2,1)} async-done(((bf16[768,384]{1,0:T(8,128)(2,1)}), bf16[192,384]{1,0:T(8,128)(2,1)}) %reduce-scatter.16.cloned.1.call-update) | async-done | bytes 147472 | tf_op jit(solution)/shard_map/reduce_scatter | solution.py:330
  818.3 40.7 %reduce-scatter.20.cloned.1.call-done = bf16[192,1536]{1,0:T(8,128)(2,1)} async-done(((bf16[768,1536]{1,0:T(8,128)(2,1)}), bf16[192,1536]{1,0:T(8,128)(2,1)}) %reduce-scatter.20.cloned.1.call-update) | async-done | bytes 589840 | tf_op jit(solution)/shard_map/reduce_scatter | solution.py:336
  859.0 59.8 %reduce-scatter.18.cloned.1.call-done = bf16[192,2,1536]{2,0,1:T(8,128)(2,1)} async-done(((bf16[768,2,1536]{2,0,1:T(8,128)(2,1)}), bf16[192,2,1536]{2,0,1:T(8,128)(2,1)}) %reduce-scatter.18.cloned.1.call-update) | async-done | bytes 1179664 | tf_op jit(solution)/shard_map/reduce_scatter | solution.py:333
  920.3 79.8 %all-reduce = (f32[384]{0:T(512)}, f32[384]{0:T(512)}, f32[768]{0:T(1024)}, f32[768]{0:T(1024)}, f32[768]{0:T(1024)}, /*index=5*/f32[768]{0:T(1024)}, f32[768]{0:T(1024)}, f32[768]{0:T(1024)}) all-reduce(f32[384]{0:T(512)S(1)} %reduce_sum.208, ...), channel_id=1, replica_groups=mesh['fsdp'=4,'ctx'=4,'tp'=2] {'fsdp','ctx'}, use_global_device_ids=true, to_apply=%region_32.33 | all-reduce | flops 5376 | bytes 43008 | tf_op jit(solution)/shard_map/psum | solution.py:357
  1003.5 19.6 %all-reduce.16.cloned.1.call-done = (bf16[192,384]{0,1:T(8,128)(2,1)}, bf16[192,384]{0,1:T(8,128)(2,1)}, bf16[192,384]{0,1:T(8,128)(2,1)}, bf16[192,2,1536]{2,0,...) async-done(((bf16[192,384]{0,1:T(8,128)(2,1)}, bf16[192,384]{0,1:T(8,128)(2,1)}, bf16[192,384]{0,1:T(8,128)(2,1)}, bf16[192,2,1536]{2,0,1:T(8,128)(2,1)}, ...) | async-done | bytes 2359312 | tf_op jit(solution)/shard_map/psum | solution.py:341
  1023.1 4.0 copy.107
  (351 shorter events, 168.1 us)
Async XLA Ops:
  8.0 25.4 %copy-start.6 = (bf16[2,512,768]{2,1,0:T(8,128)(2,1)S(1)}, bf16[2,512,768]{2,1,0:T(8,128)(2,1)}, u32[]{:S(2)}) copy-start(bf16[2,512,768]{2,1,0:T(8,128)(2,1)} %param.26) | copy-start | bytes 4718596
  8.0 25.4 %copy-start.43 = (f32[384]{0:T(512)S(1)}, f32[384]{0:T(512)}, u32[]{:S(2)}) copy-start(f32[384]{0:T(512)} %param.33) | copy-start | bytes 4612
  8.0 143.6 %all-gather.4.cloned.1.call-start = ((), (), s32[]{:S(2)}) async-start(), calls=%async_computation.7 | async-start | bytes 7864320 | tf_op jit(solution)/shard_map/all_gather | solution.py:176
  20.5 12.9 %copy-start.18 = (bf16[768,384]{1,0:T(8,128)(2,1)}, bf16[768,384]{1,0:T(8,128)(2,1)S(1)}, u32[]{:S(2)}) copy-start(bf16[768,384]{1,0:T(8,128)(2,1)S(1)} %all_gather.28) | copy-start | bytes 1769476
  30.9 2.5 copy-start.19
  34.4 12.1 %copy-start.44 = (f32[384]{0:T(512)S(1)}, f32[384]{0:T(512)}, u32[]{:S(2)}) copy-start(f32[384]{0:T(512)} %param.30) | copy-start | bytes 4612
  35.7 225.3 %all-reduce.8.cloned.1.call-start = ((), (), s32[]{:S(2)}) async-start(), calls=%async_computation.8 | async-start | bytes 3145728 | tf_op jit(solution)/shard_map/psum | solution.py:213
  47.5 14.5 %copy-start.26 = (bf16[192,384]{1,0:T(8,128)(2,1)S(1)}, bf16[192,384]{1,0:T(8,128)(2,1)}, u32[]{:S(2)}) copy-start(bf16[192,384]{1,0:T(8,128)(2,1)} %param.34) | copy-start | bytes 442372
  159.6 5.8 slice-start
  159.6 5.8 slice-start.1
  181.1 5.8 slice-start
  181.1 5.8 slice-start.1
  202.6 5.8 slice-start
  202.6 5.8 slice-start.1
  224.1 5.8 slice-start
  224.1 5.8 slice-start.1
  237.9 2.1 copy-start.14
  242.1 18.8 %copy-start.29 = (f32[768]{0:T(1024)S(1)}, f32[768]{0:T(1024)}, u32[]{:S(2)}) copy-start(f32[768]{0:T(1024)} %param.35) | copy-start | bytes 9220
  242.2 58.2 %all-gather.6.cloned.1.call-start = ((), (), s32[]{:S(2)}) async-start(), calls=%async_computation.9 | async-start | bytes 5898240 | tf_op jit(solution)/shard_map/all_gather | solution.py:219
  244.6 94.9 %all-gather.8.cloned.1.call-start = ((), (), s32[]{:S(2)}) async-start(), calls=%async_computation.10 | async-start | bytes 2949120 | tf_op jit(solution)/shard_map/all_gather | solution.py:220
  245.2 121.3 %all-reduce.10.cloned.1.call-start = ((), (), s32[]{:S(2)}) async-start(), calls=%async_computation.11 | async-start | bytes 3145728 | tf_op jit(solution)/shard_map/psum | solution.py:230
  261.0 2.6 copy-start.7
  261.0 2.8 copy-start.9
  264.7 35.7 %copy-start.27 = (f32[768]{0:T(1024)S(1)}, f32[768]{0:T(1024)}, u32[]{:S(2)}) copy-start(f32[768]{0:T(1024)} %param.36) | copy-start | bytes 9220
  264.7 35.6 %copy-start.39 = (f32[768]{0:T(1024)S(1)}, f32[768]{0:T(1024)}, u32[]{:S(2)}) copy-start(f32[768]{0:T(1024)} %param.37) | copy-start | bytes 9220
  308.2 4.7 copy-start.11
  339.6 6.7 copy-start.30
  346.0 20.6 %copy-start.37 = (f32[768]{0:T(1024)S(1)}, f32[768]{0:T(1024)}, u32[]{:S(2)}) copy-start(f32[768]{0:T(1024)} %param.40) | copy-start | bytes 9220
  346.0 71.0 %all-reduce.12.cloned.1.call-start = ((), (), s32[]{:S(2)}) async-start(), calls=%async_computation.12 | async-start | bytes 3145728 | tf_op jit(solution)/shard_map/psum | solution.py:244
  366.6 8.7 slice-start.2
  369.8 5.5 slice-start.3
  370.3 2.6 copy-start.38
  372.9 2.6 slice-start.4
  375.3 10.4 %copy-start.4 = (f32[1024,768]{1,0:T(8,128)}, f32[1024,768]{1,0:T(8,128)S(1)}, u32[]{:S(2)}) copy-start(f32[1024,768]{1,0:T(8,128)S(1)} %get-tuple-element.1416) | copy-start | bytes 9437188
  395.2 305.5 %reduce-scatter.14.cloned.1.call-start = ((), (), s32[]{:S(2)}) async-start(), calls=%async_computation.13 | async-start | bytes 7864320 | tf_op jit(solution)/shard_map/reduce_scatter | solution.py:301
  417.0 6.1 copy-start.3
  417.0 6.1 copy-start.5
  417.0 6.5 copy-start.12
  423.4 3.4 copy-start.15
  438.5 4.8 copy-start
  588.6 149.4 %reduce-scatter.22.cloned.1.call-start = ((), (), s32[]{:S(2)}) async-start(), calls=%async_computation.18 | async-start | bytes 737280
  588.9 111.8 %copy-start.8 = (bf16[2,512,768]{2,1,0:T(8,128)(2,1)S(1)}, bf16[2,512,768]{2,1,0:T(8,128)(2,1)}, u32[]{:S(2)}) copy-start(bf16[2,512,768]{2,1,0:T(8,128)(2,1)} %param.26) | copy-start | bytes 4718596
  591.9 112.3 %copy-start.16 = (bf16[1024,384]{1,0:T(8,128)(2,1)}, bf16[1024,384]{1,0:T(8,128)(2,1)S(1)}, u32[]{:S(2)}) copy-start(bf16[1024,384]{1,0:T(8,128)(2,1)S(1)} %copy.102) | copy-start | bytes 2359300
  705.4 6.8 copy-start.2
  707.7 54.1 %reduce-scatter.24.cloned.1.call-start = ((), (), s32[]{:S(2)}) async-start(), calls=%async_computation.19 | async-start | bytes 737280
  710.0 80.0 %reduce-scatter.26.cloned.1.call-start = ((), (), s32[]{:S(2)}) async-start(), calls=%async_computation.20 | async-start | bytes 737280
  712.2 106.1 %reduce-scatter.16.cloned.1.call-start = ((), (), s32[]{:S(2)}) async-start(), calls=%async_computation.15 | async-start | bytes 737280 | tf_op jit(solution)/shard_map/reduce_scatter | solution.py:330
  715.2 7.1 copy-start.28
  715.2 7.1 copy-start.40
  715.3 143.8 %reduce-scatter.20.cloned.1.call-start = ((), (), s32[]{:S(2)}) async-start(), calls=%async_computation.17 | async-start | bytes 2949120 | tf_op jit(solution)/shard_map/reduce_scatter | solution.py:336
  722.2 196.6 %reduce-scatter.18.cloned.1.call-start = ((), (), s32[]{:S(2)}) async-start(), calls=%async_computation.16 | async-start | bytes 5898240 | tf_op jit(solution)/shard_map/reduce_scatter | solution.py:333
  732.1 268.0 %all-reduce.14.cloned.1.call-start = ((), (), s32[]{:S(2)}) async-start(), calls=%async_computation.14 | async-start | bytes 3145728 | tf_op jit(solution)/shard_map/psum | solution.py:314
  737.7 182.5 %copy-start.31 = (f32[768]{0:T(1024)S(1)}, f32[768]{0:T(1024)}, u32[]{:S(2)}) copy-start(f32[768]{0:T(1024)} %get-tuple-element.1392) | copy-start | bytes 9220
  737.7 182.5 %copy-start.32 = (f32[768]{0:T(1024)S(1)}, f32[768]{0:T(1024)}, u32[]{:S(2)}) copy-start(f32[768]{0:T(1024)} %get-tuple-element.1326) | copy-start | bytes 9220
  737.7 182.5 %copy-start.33 = (f32[768]{0:T(1024)S(1)}, f32[768]{0:T(1024)}, u32[]{:S(2)}) copy-start(f32[768]{0:T(1024)} %get-tuple-element.1319) | copy-start | bytes 9220
  737.7 182.6 %copy-start.34 = (f32[768]{0:T(1024)S(1)}, f32[768]{0:T(1024)}, u32[]{:S(2)}) copy-start(f32[768]{0:T(1024)} %get-tuple-element.1324) | copy-start | bytes 9220
  737.7 182.6 %copy-start.35 = (f32[768]{0:T(1024)S(1)}, f32[768]{0:T(1024)}, u32[]{:S(2)}) copy-start(f32[768]{0:T(1024)} %get-tuple-element.1325) | copy-start | bytes 9220
  737.7 182.6 %copy-start.36 = (f32[768]{0:T(1024)S(1)}, f32[768]{0:T(1024)}, u32[]{:S(2)}) copy-start(f32[768]{0:T(1024)} %get-tuple-element.1321) | copy-start | bytes 9220
  737.7 285.4 %all-reduce.16.cloned.1.call-start = ((), (), s32[]{:S(2)}) async-start(), calls=%async_computation.21 | async-start | bytes 5013504 | tf_op jit(solution)/shard_map/psum | solution.py:341
  1023.1 4.0 copy-start.17
  1023.1 5.2 copy-start.24
  1023.1 5.9 copy-start.23
  1023.1 6.7 copy-start.22
  1023.1 7.6 copy-start.21
  (7 other events, 8.8 us)
Sparse Core Ops, SparseCore 0:
  35.8 115.7 all-gather.3
  242.3 18.6 all-reduce.7
  346.1 20.3 all-reduce.9
  395.4 21.5 all-reduce.11
  588.7 111.9 reduce-scatter.13
  737.9 20.9 all-reduce.13
  919.0 104.1 all-reduce.15
Sparse Core Ops, SparseCore 1:
  245.2 55.1 all-gather.5
  302.2 37.3 all-gather.7
  707.8 25.7 reduce-scatter.21
  736.7 25.1 reduce-scatter.23
  764.8 25.1 reduce-scatter.25
  793.1 25.1 reduce-scatter.15
  821.8 37.2 reduce-scatter.19
  861.9 56.9 reduce-scatter.17
where the time goes:
time: 1040 us
  waiting for transfers between devices  483 us (46%)
  matrix products  217 us (21%)
  blocking collectives  137 us (13%)
  other arithmetic  104 us (10%)
  local copies, waits for them, and re-layouts  73.4 us (7%)
  between operations  16.5 us (2%)
    reduce_scatter x1, waiting for transfers between devices, per_device(): lax.psum_scatter(key_terms.astype(jnp.bfloat16), 'ctx', scatter_dimension...  109 us
    psum x1, blocking collectives, per_device(): lax.psum((d_b_query, d_b_value, d_b_out, d_b_down, d_gain_one, d_shift_on...  79.8 us
    all_gather x1, waiting for transfers between devices, per_device(): pairs = lax.all_gather(key_value, 'ctx', axis=1, tiled=True)  78.7 us
    reduce_scatter x1, waiting for transfers between devices, per_device(): lax.psum_scatter(d_w_up.astype(jnp.bfloat16), 'fsdp', scatter_dimension=0...  59.8 us
    unnamed x18, waiting for transfers between devices  49.2 us
    dot_general x8, matrix products, score_block(): jnp.einsum('sqhd,skhd->shqk', query_heads, key_heads, preferred_element_t...  48.4 us
    reduce_scatter x1, waiting for transfers between devices, per_device(): lax.psum_scatter(d_w_down.astype(jnp.bfloat16), 'fsdp', scatter_dimension...  40.7 us
    all_gather x1, waiting for transfers between devices, per_device(): lax.all_gather(w_up, 'fsdp', axis=0, tiled=True)  33.3 us
  transfers between devices with their start and end apart: 15, of which 13 were waited for; matrix products, arithmetic and copies ran while one was open for 8% of the time, Pallas kernels for 0%

commit v1 on v0

--- a/solution.py
+++ b/solution.py
@@ -355,8 +355,20 @@
         total_gain_two,
         total_shift_two,
     ) = lax.psum(
-        (d_b_query, d_b_value, d_b_out, d_b_down, d_gain_one, d_shift_one, d_gain_two, d_shift_two),
-        ("fsdp", "ctx"),
+        lax.psum(
+            (
+                d_b_query,
+                d_b_value,
+                d_b_out,
+                d_b_down,
+                d_gain_one,
+                d_shift_one,
+                d_gain_two,
+                d_shift_two,
+            ),
+            "ctx",
+        ),
+        "fsdp",
     )
     return (
         result.reshape(seq_count, block_rows, model_width).astype(jnp.bfloat16),

time: 1040 us -> 1030 us (level)
  blocking collectives: 137 us -> 92.7 us
  waiting for transfers between devices: 483 us -> 526 us
  matrix products: 217 us -> 206 us
    psum x1, blocking collectives: 79.8 us -> 19.8 us  [per_device(): lax.psum((d_b_query, d_b_value, d_b_out, d_b_down, d_gain_one, d_shift_on...]
    psum x1, waiting for transfers between devices: 19.6 us -> 62.5 us  [per_device(): lax.psum(shard_grads[0].astype(jnp.bfloat16), 'ctx').astype(jnp.float32)]
    psum x0 -> x1, blocking collectives: none -> 16.1 us  [per_device(): lax.psum(lax.psum((d_b_query, d_b_value, d_b_out, d_b_down, d_gain_one, d...]
    unnamed x112 -> x124, local copies, waits for them, and re-layouts: 33.1 us -> 31.4 us
  transfers between devices with their start and end apart: 15 -> 15, of which waited for: 13 -> 13; matrix products, arithmetic and copies ran while one was open for 8% -> 7% of each run, Pallas kernels for 0% -> 0%
where the time goes in v1:
time: 1030 us
  waiting for transfers between devices  526 us (51%)
  matrix products  206 us (20%)
  other arithmetic  101 us (10%)
  blocking collectives  92.7 us (9%)
  local copies, waits for them, and re-layouts  75.8 us (7%)
  between operations  16.6 us (2%)
    reduce_scatter x1, waiting for transfers between devices, per_device(): lax.psum_scatter(key_terms.astype(jnp.bfloat16), 'ctx', scatter_dimension...  109 us
    all_gather x1, waiting for transfers between devices, per_device(): pairs = lax.all_gather(key_value, 'ctx', axis=1, tiled=True)  78.7 us
    psum x1, waiting for transfers between devices, per_device(): lax.psum(shard_grads[0].astype(jnp.bfloat16), 'ctx').astype(jnp.float32)  62.5 us
    reduce_scatter x1, waiting for transfers between devices, per_device(): lax.psum_scatter(d_w_up.astype(jnp.bfloat16), 'fsdp', scatter_dimension=0...  59.8 us
    unnamed x18, waiting for transfers between devices  49.5 us
    dot_general x8, matrix products, score_block(): jnp.einsum('sqhd,skhd->shqk', query_heads, key_heads, preferred_element_t...  48.4 us
    reduce_scatter x1, waiting for transfers between devices, per_device(): lax.psum_scatter(d_w_down.astype(jnp.bfloat16), 'fsdp', scatter_dimension...  40.8 us
    all_gather x1, waiting for transfers between devices, per_device(): lax.all_gather(w_up, 'fsdp', axis=0, tiled=True)  33.3 us
  transfers between devices with their start and end apart: 15, of which 13 were waited for; matrix products, arithmetic and copies ran while one was open for 7% of the time, Pallas kernels for 0%

profile of v1, /device:TPU:0, one launch (start us, length us, event | category | flops | bytes accessed | tf_op | source)
XLA Modules:
  0.0 1027.4 jit_solution(4645251976995672233)
XLA Ops:
  8.1 12.4 %all_gather.28 = bf16[768,384]{1,0:T(8,128)(2,1)S(1)} all-gather(bf16[192,384]{1,0:T(8,128)(2,1)} %param.32), channel_id=1, replica_groups=mesh['fsdp'=4,'ctx'=4,'tp'=2] {'fsdp'}, dimensions={0}, use_global_device_ids=true | all-gather | bytes 737280 | tf_op jit(solution)/shard_map/all_gather | solution.py:140
  20.5 10.4 %all_gather.27 = bf16[768,384]{1,0:T(8,128)(2,1)S(1)} all-gather(bf16[192,384]{1,0:T(8,128)(2,1)} %param.31), channel_id=1, replica_groups=mesh['fsdp'=4,'ctx'=4,'tp'=2] {'fsdp'}, dimensions={0}, use_global_device_ids=true | all-gather | bytes 737280 | tf_op jit(solution)/shard_map/all_gather | solution.py:139
  36.0 9.7 all_gather.30
  48.5 13.5 %all_gather.26 = s32[2,2048]{1,0:T(2,128)S(1)} all-gather(s32[2,512]{1,0:T(2,128)S(1)} %copy-done.49), channel_id=1, replica_groups=mesh['fsdp'=4,'ctx'=4,'tp'=2] {'ctx'}, dimensions={1}, use_global_device_ids=true | all-gather | bytes 20480 | tf_op jit(solution)/shard_map/all_gather | solution.py:177
  62.0 10.8 %all_gather.31 = bf16[768,384]{1,0:T(8,128)(2,1)} all-gather(bf16[192,384]{1,0:T(8,128)(2,1)S(1)} %copy-done.34), channel_id=1, replica_groups=mesh['fsdp'=4,'ctx'=4,'tp'=2] {'fsdp'}, dimensions={0}, use_global_device_ids=true | all-gather | bytes 737280 | tf_op jit(solution)/shard_map/all_gather | solution.py:141
  72.9 78.7 %all-gather.4.cloned.1.call-done = bf16[2,2048,768]{1,2,0:T(8,128)(2,1)} async-done(((bf16[2,512,768]{1,2,0:T(8,128)(2,1)}), bf16[2,2048,768]{1,2,0:T(8,128)(2,1)}) %all-gather.4.cloned.1.call-update) | async-done | bytes 6291472 | tf_op jit(solution)/shard_map/all_gather | solution.py:176
  151.8 86.0 %while.38 = (s32[]{:T(128)}, f32[2,6,512]{2,1,0:T(8,128)S(1)}, f32[2,6,512]{2,1,0:T(8,128)S(1)}, f32[2,6,512,64]{2,3,1,0:T(8,128)S(1)}, s32[2,1,8]{2,0,1:T(2,128...) while((s32[]{:T(128)}, f32[2,6,512]{2,1,0:T(8,128)S(1)}, ...), condition=%wide.region_9.10_spmd.clone, body=%wide.region_2.9_spmd.clone.sunk | while | flops 860657216 | bytes 95593216 | solution.py:101
  153.4 20.0 %conditional.6 = ((f32[2,6,512]{2,1,0:T(8,128)S(1)}, f32[2,6,512]{2,1,0:T(8,128)S(1)}, f32[2,6,512,64]{2,3,1,0:T(8,128)S(1)})) conditional(s32[]{:T(128)} %convert_element_type.410, (f32[2,6,512]{2,1,0:T(8,128)S(1)}, f32[2,6,512]{2,1,0:T(8,128)S(1)}, f32[2,6,512,64]{2,3,1,0:T(8,128)S(1)}) %tuple.180, (s32[2,512]{1,0:T(2,128)S(1)}, ...), branch_computations={%region_5.5_spmd, %region_6.8_spmd.clone} | conditional | flops 860633152 | bytes 95582496 | solution.py:95
  159.6 5.7 fusion.11
  165.4 3.8 fusion.10
  169.2 4.1 multiply_add_fusion
  174.9 20.0 %conditional.6 = ((f32[2,6,512]{2,1,0:T(8,128)S(1)}, f32[2,6,512]{2,1,0:T(8,128)S(1)}, f32[2,6,512,64]{2,3,1,0:T(8,128)S(1)})) conditional(s32[]{:T(128)} %convert_element_type.410, (f32[2,6,512]{2,1,0:T(8,128)S(1)}, f32[2,6,512]{2,1,0:T(8,128)S(1)}, f32[2,6,512,64]{2,3,1,0:T(8,128)S(1)}) %tuple.180, (s32[2,512]{1,0:T(2,128)S(1)}, ...), branch_computations={%region_5.5_spmd, %region_6.8_spmd.clone} | conditional | flops 860633152 | bytes 95582496 | solution.py:95
  181.1 5.7 fusion.11
  190.7 4.1 multiply_add_fusion
  196.4 20.0 %conditional.6 = ((f32[2,6,512]{2,1,0:T(8,128)S(1)}, f32[2,6,512]{2,1,0:T(8,128)S(1)}, f32[2,6,512,64]{2,3,1,0:T(8,128)S(1)})) conditional(s32[]{:T(128)} %convert_element_type.410, (f32[2,6,512]{2,1,0:T(8,128)S(1)}, f32[2,6,512]{2,1,0:T(8,128)S(1)}, f32[2,6,512,64]{2,3,1,0:T(8,128)S(1)}) %tuple.180, (s32[2,512]{1,0:T(2,128)S(1)}, ...), branch_computations={%region_5.5_spmd, %region_6.8_spmd.clone} | conditional | flops 860633152 | bytes 95582496 | solution.py:95
  202.6 5.7 fusion.11
  212.2 4.1 multiply_add_fusion
  217.9 20.0 %conditional.6 = ((f32[2,6,512]{2,1,0:T(8,128)S(1)}, f32[2,6,512]{2,1,0:T(8,128)S(1)}, f32[2,6,512,64]{2,3,1,0:T(8,128)S(1)})) conditional(s32[]{:T(128)} %convert_element_type.410, (f32[2,6,512]{2,1,0:T(8,128)S(1)}, f32[2,6,512]{2,1,0:T(8,128)S(1)}, f32[2,6,512,64]{2,3,1,0:T(8,128)S(1)}) %tuple.180, (s32[2,512]{1,0:T(2,128)S(1)}, ...), branch_computations={%region_5.5_spmd, %region_6.8_spmd.clone} | conditional | flops 860633152 | bytes 95582496 | solution.py:95
  224.1 5.7 fusion.11
  233.7 4.1 multiply_add_fusion
  245.5 15.5 %all-reduce.9.cloned.1.call-done = bf16[1024,768]{1,0:T(8,128)(2,1)} async-done(((bf16[1024,768]{1,0:T(8,128)(2,1)}), bf16[1024,768]{1,0:T(8,128)(2,1)}) %all-reduce.9.cloned.1.call-update) | async-done | bytes 1572880 | tf_op jit(solution)/shard_map/psum | solution.py:213
  267.1 33.3 %all-gather.6.cloned.1.call-done = bf16[768,2,1536]{2,0,1:T(8,128)(2,1)} async-done(((bf16[192,2,1536]{2,0,1:T(8,128)(2,1)}), bf16[768,2,1536]{2,0,1:T(8,128)(2,1)}) %all-gather.6.cloned.1.call-update) | async-done | bytes 4718608 | tf_op jit(solution)/shard_map/all_gather | solution.py:219
  300.3 7.8 fusion.80
  308.2 4.7 copy-done.13
  312.9 14.8 %multiply_convert_fusion.1 = (bf16[1024,1536]{1,0:T(8,128)(2,1)}, f32[1024,1536]{1,0:T(8,128)}) fusion(f32[1024,2,1536]{2,0,1:T(8,128)S(1)} %fusion.80), kind=kLoop, calls=%fused_computation.88 | loop fusion | flops 103809024 | bytes 22020096 | tf_op jit(solution)/shard_map/convert_element_type | solution.py:228
  327.6 11.9 %all-gather.8.cloned.1.call-done = bf16[768,1536]{1,0:T(8,128)(2,1)} async-done(((bf16[192,1536]{1,0:T(8,128)(2,1)}), bf16[768,1536]{1,0:T(8,128)(2,1)}) %all-gather.8.cloned.1.call-update) | async-done | bytes 2359312 | tf_op jit(solution)/shard_map/all_gather | solution.py:220
  339.5 6.4 convolution_convert_fusion.4
  349.0 17.5 %all-reduce.11.cloned.1.call-done = bf16[1024,768]{1,0:T(8,128)(2,1)} async-done(((bf16[1024,768]{1,0:T(8,128)(2,1)}), bf16[1024,768]{1,0:T(8,128)(2,1)}) %all-reduce.11.cloned.1.call-update) | async-done | bytes 1572880 | tf_op jit(solution)/shard_map/psum | solution.py:230
  375.5 10.2 fusion.65
  385.7 9.5 bitcast_convert_fusion
  395.7 21.2 %all-reduce.13.cloned.1.call-done = bf16[1024,768]{1,0:T(8,128)(2,1)} async-done(((bf16[1024,768]{1,0:T(8,128)(2,1)}), bf16[1024,768]{1,0:T(8,128)(2,1)}) %all-reduce.13.cloned.1.call-update) | async-done | bytes 1572880 | tf_op jit(solution)/shard_map/psum | solution.py:244
  416.9 6.1 multiply_reduce_fusion
  438.2 133.5 %while.39 = (s32[]{:T(128)}, f32[2,512,6,64]{1,3,2,0:T(8,128)}, bf16[2,2048,768]{1,2,0:T(8,128)(2,1)}, s32[2,1,8]{2,0,1:T(2,128)S(1)}, s32[2,512]{1,0:T(2,128)S(...) while((s32[]{:T(128)}, f32[2,512,6,64]{1,3,2,0:T(8,128)}, ...), condition=%wide.region_26.27_spmd.clone, body=%wide.region_21.0_spmd.clone.sunk | while | flops 2059953664 | bytes 108905248 | solution.py:101
  439.9 31.9 %conditional.7 = ((f32[2,512,6,64]{1,3,2,0:T(8,128)}, bf16[2,2048,768]{1,2,0:T(8,128)(2,1)})) conditional(s32[]{:T(128)} %convert_element_type.412, (f32[2,512,6,64]{1,3,2,0:T(8,128)}, bf16[2,2048,768]{1,2,0:T(8,128)(2,1)}) %tuple.184, (s32[2,512]{1,0:T(2,128)S(1)}, s32[2,512]{1,0:T(2,128)S(1)}, s32[]{:T(128)}, s32[2,2048]{1,0:T(2,128)S(1)}, ...), branch_computations={%region_24.24_spmd, %region_25.25_spmd.clone} | conditional | flops 2059929600 | bytes 108894504 | solution.py:95
  443.2 6.4 fusion.98
  450.8 8.2 fusion.23
  461.0 6.5 fusion.28
  473.3 31.9 %conditional.7 = ((f32[2,512,6,64]{1,3,2,0:T(8,128)}, bf16[2,2048,768]{1,2,0:T(8,128)(2,1)})) conditional(s32[]{:T(128)} %convert_element_type.412, (f32[2,512,6,64]{1,3,2,0:T(8,128)}, bf16[2,2048,768]{1,2,0:T(8,128)(2,1)}) %tuple.184, (s32[2,512]{1,0:T(2,128)S(1)}, s32[2,512]{1,0:T(2,128)S(1)}, s32[]{:T(128)}, s32[2,2048]{1,0:T(2,128)S(1)}, ...), branch_computations={%region_24.24_spmd, %region_25.25_spmd.clone} | conditional | flops 2059929600 | bytes 108894504 | solution.py:95
  476.6 6.4 fusion.98
  484.2 8.2 fusion.23
  494.4 6.5 fusion.28
  506.6 31.9 %conditional.7 = ((f32[2,512,6,64]{1,3,2,0:T(8,128)}, bf16[2,2048,768]{1,2,0:T(8,128)(2,1)})) conditional(s32[]{:T(128)} %convert_element_type.412, (f32[2,512,6,64]{1,3,2,0:T(8,128)}, bf16[2,2048,768]{1,2,0:T(8,128)(2,1)}) %tuple.184, (s32[2,512]{1,0:T(2,128)S(1)}, s32[2,512]{1,0:T(2,128)S(1)}, s32[]{:T(128)}, s32[2,2048]{1,0:T(2,128)S(1)}, ...), branch_computations={%region_24.24_spmd, %region_25.25_spmd.clone} | conditional | flops 2059929600 | bytes 108894504 | solution.py:95
  509.9 6.4 fusion.98
  517.5 8.2 fusion.23
  527.7 6.5 fusion.28
  539.9 31.9 %conditional.7 = ((f32[2,512,6,64]{1,3,2,0:T(8,128)}, bf16[2,2048,768]{1,2,0:T(8,128)(2,1)})) conditional(s32[]{:T(128)} %convert_element_type.412, (f32[2,512,6,64]{1,3,2,0:T(8,128)}, bf16[2,2048,768]{1,2,0:T(8,128)(2,1)}) %tuple.184, (s32[2,512]{1,0:T(2,128)S(1)}, s32[2,512]{1,0:T(2,128)S(1)}, s32[]{:T(128)}, s32[2,2048]{1,0:T(2,128)S(1)}, ...), branch_computations={%region_24.24_spmd, %region_25.25_spmd.clone} | conditional | flops 2059929600 | bytes 108894504 | solution.py:95
  543.2 6.4 fusion.98
  550.8 8.2 fusion.23
  561.0 6.5 fusion.28
  571.8 8.6 copy.101
  583.3 109.2 %reduce-scatter.14.cloned.1.call-done = bf16[2,512,768]{2,1,0:T(8,128)(2,1)} async-done(((bf16[2,2048,768]{2,1,0:T(8,128)(2,1)}), bf16[2,512,768]{2,1,0:T(8,128)(2,1)}) %reduce-scatter.14.cloned.1.call-update) | async-done | bytes 1572880 | tf_op jit(solution)/shard_map/reduce_scatter | solution.py:301
  703.4 7.0 convolution_convert_fusion.1
  710.5 9.7 convolution_convert_fusion
  721.9 4.8 fusion.75
  729.0 22.3 %reduce-scatter.24.cloned.1.call-done = bf16[192,384]{1,0:T(8,128)(2,1)} async-done(((bf16[768,384]{1,0:T(8,128)(2,1)}), bf16[192,384]{1,0:T(8,128)(2,1)}) %reduce-scatter.24.cloned.1.call-update) | async-done | bytes 147472
  753.1 26.3 %reduce-scatter.26.cloned.1.call-done = bf16[192,384]{1,0:T(8,128)(2,1)} async-done(((bf16[768,384]{1,0:T(8,128)(2,1)}), bf16[192,384]{1,0:T(8,128)(2,1)}) %reduce-scatter.26.cloned.1.call-update) | async-done | bytes 147472
  781.1 26.6 %reduce-scatter.16.cloned.1.call-done = bf16[192,384]{1,0:T(8,128)(2,1)} async-done(((bf16[768,384]{1,0:T(8,128)(2,1)}), bf16[192,384]{1,0:T(8,128)(2,1)}) %reduce-scatter.16.cloned.1.call-update) | async-done | bytes 147472 | tf_op jit(solution)/shard_map/reduce_scatter | solution.py:330
  807.7 40.8 %reduce-scatter.20.cloned.1.call-done = bf16[192,1536]{1,0:T(8,128)(2,1)} async-done(((bf16[768,1536]{1,0:T(8,128)(2,1)}), bf16[192,1536]{1,0:T(8,128)(2,1)}) %reduce-scatter.20.cloned.1.call-update) | async-done | bytes 589840 | tf_op jit(solution)/shard_map/reduce_scatter | solution.py:336
  848.5 59.8 %reduce-scatter.18.cloned.1.call-done = bf16[192,2,1536]{2,0,1:T(8,128)(2,1)} async-done(((bf16[768,2,1536]{2,0,1:T(8,128)(2,1)}), bf16[192,2,1536]{2,0,1:T(8,128)(2,1)}) %reduce-scatter.18.cloned.1.call-update) | async-done | bytes 1179664 | tf_op jit(solution)/shard_map/reduce_scatter | solution.py:333
  908.6 19.8 %all-reduce = (f32[384]{0:T(512)S(1)}, f32[384]{0:T(512)S(1)}, f32[768]{0:T(1024)S(1)}, f32[768]{0:T(1024)S(1)}, f32[768]{0:T(1024)S(1)}, /*index=5*/f32[768]{0:T(1024)S(1)}, f32[768]{0:T(1024)S(1)}, f32[768]{0:T(1024)S(1)}) all-reduce(f32[384]{0:T(512)S(1)} %reduce_sum.208, ...), channel_id=1, replica_groups=mesh['fsdp'=4,'ctx'=4,'tp'=2] {'ctx'}, use_global_device_ids=true, to_apply=%region_32.33 | all-reduce | flops 5376 | bytes 43008 | tf_op jit(solution)/shard_map/psum | solution.py:358
  928.4 16.1 %all-reduce.1 = (f32[384]{0:T(512)}, f32[384]{0:T(512)}, f32[768]{0:T(1024)}, f32[768]{0:T(1024)}, f32[768]{0:T(1024)}, /*index=5*/f32[768]{0:T(1024)}, f32[768]{0:T(1024)}, f32[768]{0:T(1024)}) all-reduce(f32[384]{0:T(512)S(1)} %get-tuple-element.1376, ...), channel_id=1, replica_groups=mesh['fsdp'=4,'ctx'=4,'tp'=2] {'fsdp'}, use_global_device_ids=true, to_apply=%region_33.34 | all-reduce | flops 5376 | bytes 43008 | tf_op jit(solution)/shard_map/psum | solution.py:357
  944.4 4.3 convert_add_fusion
  948.8 62.5 %all-reduce.17.cloned.1.call-done = (bf16[192,384]{0,1:T(8,128)(2,1)}, bf16[192,384]{0,1:T(8,128)(2,1)}, bf16[192,384]{0,1:T(8,128)(2,1)}, bf16[192,2,1536]{2,0,...) async-done(((bf16[192,384]{0,1:T(8,128)(2,1)}, bf16[192,384]{0,1:T(8,128)(2,1)}, bf16[192,384]{0,1:T(8,128)(2,1)}, bf16[192,2,1536]{2,0,1:T(8,128)(2,1)}, ...) | async-done | bytes 2359312 | tf_op jit(solution)/shard_map/psum | solution.py:341
  1011.3 4.0 copy.107
  (380 shorter events, 160.5 us)
Async XLA Ops:
  8.0 25.4 %copy-start.8 = (bf16[2,512,768]{2,1,0:T(8,128)(2,1)S(1)}, bf16[2,512,768]{2,1,0:T(8,128)(2,1)}, u32[]{:S(2)}) copy-start(bf16[2,512,768]{2,1,0:T(8,128)(2,1)} %param.26) | copy-start | bytes 4718596
  8.0 25.4 %copy-start.51 = (f32[384]{0:T(512)S(1)}, f32[384]{0:T(512)}, u32[]{:S(2)}) copy-start(f32[384]{0:T(512)} %param.33) | copy-start | bytes 4612
  8.0 143.6 %all-gather.4.cloned.1.call-start = ((), (), s32[]{:S(2)}) async-start(), calls=%async_computation.7 | async-start | bytes 7864320 | tf_op jit(solution)/shard_map/all_gather | solution.py:176
  20.5 12.9 %copy-start.22 = (bf16[768,384]{1,0:T(8,128)(2,1)}, bf16[768,384]{1,0:T(8,128)(2,1)S(1)}, u32[]{:S(2)}) copy-start(bf16[768,384]{1,0:T(8,128)(2,1)S(1)} %all_gather.28) | copy-start | bytes 1769476
  30.9 2.5 copy-start.24
  34.4 12.1 %copy-start.52 = (f32[384]{0:T(512)S(1)}, f32[384]{0:T(512)}, u32[]{:S(2)}) copy-start(f32[384]{0:T(512)} %param.30) | copy-start | bytes 4612
  35.7 225.3 %all-reduce.9.cloned.1.call-start = ((), (), s32[]{:S(2)}) async-start(), calls=%async_computation.8 | async-start | bytes 3145728 | tf_op jit(solution)/shard_map/psum | solution.py:213
  47.5 14.5 %copy-start.34 = (bf16[192,384]{1,0:T(8,128)(2,1)S(1)}, bf16[192,384]{1,0:T(8,128)(2,1)}, u32[]{:S(2)}) copy-start(bf16[192,384]{1,0:T(8,128)(2,1)} %param.34) | copy-start | bytes 442372
  159.6 5.8 slice-start
  159.6 5.8 slice-start.1
  181.1 5.8 slice-start
  181.1 5.8 slice-start.1
  202.6 5.8 slice-start
  202.6 5.8 slice-start.1
  224.1 5.8 slice-start
  224.1 5.8 slice-start.1
  242.1 18.9 %copy-start.37 = (f32[768]{0:T(1024)S(1)}, f32[768]{0:T(1024)}, u32[]{:S(2)}) copy-start(f32[768]{0:T(1024)} %param.35) | copy-start | bytes 9220
  242.1 58.2 %all-gather.6.cloned.1.call-start = ((), (), s32[]{:S(2)}) async-start(), calls=%async_computation.9 | async-start | bytes 5898240 | tf_op jit(solution)/shard_map/all_gather | solution.py:219
  244.6 94.9 %all-gather.8.cloned.1.call-start = ((), (), s32[]{:S(2)}) async-start(), calls=%async_computation.10 | async-start | bytes 2949120 | tf_op jit(solution)/shard_map/all_gather | solution.py:220
  245.2 121.3 %all-reduce.11.cloned.1.call-start = ((), (), s32[]{:S(2)}) async-start(), calls=%async_computation.11 | async-start | bytes 3145728 | tf_op jit(solution)/shard_map/psum | solution.py:230
  261.0 2.6 copy-start.9
  261.0 2.8 copy-start.11
  264.7 35.6 %copy-start.35 = (f32[768]{0:T(1024)S(1)}, f32[768]{0:T(1024)}, u32[]{:S(2)}) copy-start(f32[768]{0:T(1024)} %param.36) | copy-start | bytes 9220
  264.7 35.6 %copy-start.47 = (f32[768]{0:T(1024)S(1)}, f32[768]{0:T(1024)}, u32[]{:S(2)}) copy-start(f32[768]{0:T(1024)} %param.37) | copy-start | bytes 9220
  308.2 4.7 copy-start.13
  339.5 6.7 copy-start.38
  346.0 20.6 %copy-start.45 = (f32[768]{0:T(1024)S(1)}, f32[768]{0:T(1024)}, u32[]{:S(2)}) copy-start(f32[768]{0:T(1024)} %param.40) | copy-start | bytes 9220
  346.0 71.0 %all-reduce.13.cloned.1.call-start = ((), (), s32[]{:S(2)}) async-start(), calls=%async_computation.12 | async-start | bytes 3145728 | tf_op jit(solution)/shard_map/psum | solution.py:244
  366.5 8.7 slice-start.2
  369.8 5.5 slice-start.3
  370.3 2.6 copy-start.46
  372.9 2.6 slice-start.4
  375.3 10.4 %copy-start.6 = (f32[1024,768]{1,0:T(8,128)}, f32[1024,768]{1,0:T(8,128)S(1)}, u32[]{:S(2)}) copy-start(f32[1024,768]{1,0:T(8,128)S(1)} %get-tuple-element.1424) | copy-start | bytes 9437188
  395.2 297.3 %reduce-scatter.14.cloned.1.call-start = ((), (), s32[]{:S(2)}) async-start(), calls=%async_computation.13 | async-start | bytes 7864320 | tf_op jit(solution)/shard_map/reduce_scatter | solution.py:301
  416.9 6.1 copy-start.5
  416.9 6.1 copy-start.7
  416.9 6.5 copy-start.14
  423.4 3.4 copy-start.18
  433.5 4.8 copy-start
  580.5 146.7 %reduce-scatter.22.cloned.1.call-start = ((), (), s32[]{:S(2)}) async-start(), calls=%async_computation.18 | async-start | bytes 737280
  582.0 110.5 %copy-start.10 = (bf16[2,512,768]{2,1,0:T(8,128)(2,1)S(1)}, bf16[2,512,768]{2,1,0:T(8,128)(2,1)}, u32[]{:S(2)}) copy-start(bf16[2,512,768]{2,1,0:T(8,128)(2,1)} %param.26) | copy-start | bytes 4718596
  583.3 109.2 %copy-start.19 = (bf16[1024,384]{1,0:T(8,128)(2,1)}, bf16[1024,384]{1,0:T(8,128)(2,1)S(1)}, u32[]{:S(2)}) copy-start(bf16[1024,384]{1,0:T(8,128)(2,1)S(1)} %copy.102) | copy-start | bytes 2359300
  696.1 3.5 copy-start.16
  697.2 54.1 %reduce-scatter.24.cloned.1.call-start = ((), (), s32[]{:S(2)}) async-start(), calls=%async_computation.19 | async-start | bytes 737280
  698.4 81.0 %reduce-scatter.26.cloned.1.call-start = ((), (), s32[]{:S(2)}) async-start(), calls=%async_computation.20 | async-start | bytes 737280
  699.5 108.2 %reduce-scatter.16.cloned.1.call-start = ((), (), s32[]{:S(2)}) async-start(), calls=%async_computation.15 | async-start | bytes 737280 | tf_op jit(solution)/shard_map/reduce_scatter | solution.py:330
  703.4 7.1 copy-start.36
  703.4 7.1 copy-start.48
  703.4 145.1 %reduce-scatter.20.cloned.1.call-start = ((), (), s32[]{:S(2)}) async-start(), calls=%async_computation.17 | async-start | bytes 2949120 | tf_op jit(solution)/shard_map/reduce_scatter | solution.py:336
  710.4 197.8 %reduce-scatter.18.cloned.1.call-start = ((), (), s32[]{:S(2)}) async-start(), calls=%async_computation.16 | async-start | bytes 5898240 | tf_op jit(solution)/shard_map/reduce_scatter | solution.py:333
  720.3 224.1 %all-reduce.15.cloned.1.call-start = ((), (), s32[]{:S(2)}) async-start(), calls=%async_computation.14 | async-start | bytes 3145728 | tf_op jit(solution)/shard_map/psum | solution.py:314
  726.7 181.6 %copy-start.28 = (bf16[2,512,768]{2,1,0:T(8,128)(2,1)S(1)}, bf16[2,512,768]{2,1,0:T(8,128)(2,1)}, u32[]{:S(2)}) copy-start(bf16[2,512,768]{2,1,0:T(8,128)(2,1)} %reduce-scatter.14.cloned.1.call-done) | copy-start | bytes 4718596
  726.7 181.8 %copy-start.39 = (f32[768]{0:T(1024)S(1)}, f32[768]{0:T(1024)}, u32[]{:S(2)}) copy-start(f32[768]{0:T(1024)} %get-tuple-element.1400) | copy-start | bytes 9220
  726.7 181.8 %copy-start.40 = (f32[768]{0:T(1024)S(1)}, f32[768]{0:T(1024)}, u32[]{:S(2)}) copy-start(f32[768]{0:T(1024)} %get-tuple-element.1326) | copy-start | bytes 9220
  726.7 181.8 %copy-start.41 = (f32[768]{0:T(1024)S(1)}, f32[768]{0:T(1024)}, u32[]{:S(2)}) copy-start(f32[768]{0:T(1024)} %get-tuple-element.1319) | copy-start | bytes 9220
  726.7 181.8 %copy-start.42 = (f32[768]{0:T(1024)S(1)}, f32[768]{0:T(1024)}, u32[]{:S(2)}) copy-start(f32[768]{0:T(1024)} %get-tuple-element.1324) | copy-start | bytes 9220
  726.7 181.8 %copy-start.43 = (f32[768]{0:T(1024)S(1)}, f32[768]{0:T(1024)}, u32[]{:S(2)}) copy-start(f32[768]{0:T(1024)} %get-tuple-element.1325) | copy-start | bytes 9220
  726.8 181.8 %copy-start.44 = (f32[768]{0:T(1024)S(1)}, f32[768]{0:T(1024)}, u32[]{:S(2)}) copy-start(f32[768]{0:T(1024)} %get-tuple-element.1321) | copy-start | bytes 9220
  726.8 284.5 %all-reduce.17.cloned.1.call-start = ((), (), s32[]{:S(2)}) async-start(), calls=%async_computation.21 | async-start | bytes 5013504 | tf_op jit(solution)/shard_map/psum | solution.py:341
  1011.3 4.0 copy-start.21
  1011.3 5.2 copy-start.32
  1011.3 5.9 copy-start.31
  1011.3 6.7 copy-start.30
  1011.3 7.6 copy-start.29
  (21 other events, 30.3 us)
Sparse Core Ops, SparseCore 0:
  35.8 115.7 all-gather.3
  242.3 18.6 all-reduce.8
  346.1 20.3 all-reduce.10
  395.3 21.5 all-reduce.12
  580.6 111.9 reduce-scatter.13
  726.9 20.9 all-reduce.14
  908.4 102.8 all-reduce.16
Sparse Core Ops, SparseCore 1:
  245.2 55.1 all-gather.5
  302.2 37.3 all-gather.7
  697.3 25.7 reduce-scatter.21
  726.2 25.1 reduce-scatter.23
  754.2 25.1 reduce-scatter.25
  782.5 25.1 reduce-scatter.15
  811.2 37.2 reduce-scatter.19
  851.3 56.9 reduce-scatter.17
